TPU v7x, 32 devices: a whole 2x2x4 slice. The times are simulated.
32 devices in a mesh: groups: 2 (over x), seq: 16 (over z, y, core).
Axes of the slice: x: 2, y: 2, z: 4, core: 2. Of those that a mesh axis runs over, the one named last changes fastest.
Arguments:
- signal: bfloat16 [32768, 768], P(('groups', 'seq')), parts along dimension 0, may hold values from -6 to 6
- norm_gain: float32 [768], replicated, may hold values from 0.1 to 1.9
- conv_weight: bfloat16 [3, 768, 384], replicated, may hold values from -0.125 to 0.125
- output_weight: bfloat16 [384, 768], replicated, may hold values from -0.3125 to 0.3125
- cotangent: bfloat16 [32768, 768], P(('groups', 'seq')), parts along dimension 0, may hold values from -6 to 6
Outputs:
- block_out: bfloat16 [32768, 768], P(('groups', 'seq')), parts along dimension 0
- signal_grad: bfloat16 [32768, 768], P(('groups', 'seq')), parts along dimension 0
- conv_grad: float32 [6, 768, 384], P('groups'), parts along dimension 0
- output_grad: float32 [768, 768], P('groups'), parts along dimension 0
There are 2 independent parts, one for each index of `groups`. A program takes and returns all parts, laid end to end along the dimension named above; an argument that names none is the same for every part. Nothing has to cross between parts.
All inputs are finite; a program needn't handle non-finite values.
Results may differ from a plain program's by a relative error of at most 0.0056.
Values may be sent and summed in bfloat16 or wider, within the bound.
A program may use at most 128 MiB of HBM per device.

v0:
```python
import math

import jax
import jax.numpy as jnp
from jax import lax
from jax.sharding import PartitionSpec as P

epsilon = 1e-06


def passed_along(block, axis, distance):
    devices = range(lax.axis_size(axis))
    route = [(i - distance, i) for i in devices if i - distance in devices]
    return lax.ppermute(block, axis, route)


def gelu_slope(value):
    return 0.5 * (1.0 + jax.scipy.special.erf(value * (1.0 / math.sqrt(2.0)))) + value * jnp.exp(
        -0.5 * value * value
    ) * (1.0 / math.sqrt(2.0 * math.pi))


def shards(signal, norm_gain, conv_weight, output_weight, cotangent):
    devices = lax.axis_size("seq")
    stride = devices // 8
    local_bins = signal.shape[0]
    signal_f = signal.astype(jnp.float32)
    mean_square = jnp.mean(signal_f * signal_f, axis=-1, keepdims=True)
    inverse_rms = lax.rsqrt(mean_square + epsilon)
    normed = signal_f * inverse_rms * norm_gain
    activated_signal = jax.nn.gelu(normed, approximate=False).astype(jnp.bfloat16)
    earlier_taps = passed_along(activated_signal, "seq", stride)
    later_taps = passed_along(activated_signal, "seq", -stride)
    stacked = jnp.stack([earlier_taps, activated_signal, later_taps])
    hidden = jnp.einsum("kbc,kch->bh", stacked, conv_weight, preferred_element_type=jnp.float32)
    gated = jax.nn.gelu(hidden, approximate=False).astype(jnp.bfloat16)
    block_out = (
        signal_f + jnp.dot(gated, output_weight, preferred_element_type=jnp.float32)
    ).astype(jnp.bfloat16)
    grad_scale = 1.0 / math.sqrt(local_bins * devices)
    gated_grad = jnp.dot(cotangent, output_weight.T, preferred_element_type=jnp.float32)
    hidden_grad = (gated_grad * gelu_slope(hidden)).astype(jnp.bfloat16)
    output_term = jnp.dot(gated.T, cotangent, preferred_element_type=jnp.float32) * grad_scale
    conv_term = (
        jnp.einsum("kbc,bh->kch", stacked, hidden_grad, preferred_element_type=jnp.float32)
        * grad_scale
    )
    tap_terms = jnp.einsum(
        "bh,kch->kbc", hidden_grad, conv_weight, preferred_element_type=jnp.float32
    )
    from_after = passed_along(tap_terms[0].astype(jnp.bfloat16), "seq", -stride).astype(jnp.float32)
    from_before = passed_along(tap_terms[2].astype(jnp.bfloat16), "seq", stride).astype(jnp.float32)
    input_gradient = tap_terms[1] + from_after + from_before
    conv_grad, output_grad = lax.psum((conv_term, output_term), "seq")
    weighted = input_gradient * gelu_slope(normed) * norm_gain
    inner = jnp.mean(weighted * signal_f, axis=-1, keepdims=True)
    cubed = inverse_rms * inverse_rms * inverse_rms
    signal_grad = cotangent.astype(jnp.float32) + weighted * inverse_rms - signal_f * cubed * inner
    return (block_out, signal_grad.astype(jnp.bfloat16), conv_grad, output_grad)


def solution(mesh):
    placed = (P(("groups", "seq"), None), P(), P(), P(), P(("groups", "seq"), None))
    return jax.shard_map(
        shards,
        mesh=mesh,
        in_specs=placed,
        out_specs=(
            P(("groups", "seq"), None),
            P(("groups", "seq"), None),
            P("groups", None, None),
            P("groups", None),
        ),
        check_vma=False,
    )
```

profile of v0, /device:TPU:31, one launch (start us, length us, event | category | flops | bytes accessed | tf_op | source)
XLA Modules:
  0.0 275.8 jit_solution(352811889934860932)
XLA Ops:
  7.2 0.0 copy-start
  7.2 0.0 all-reduce.3.cloned.1.call-start
  7.2 1.9 fusion.9
  9.2 8.7 %fusion.2 = bf16[1024,768]{1,0:T(8,128)(2,1)S(1)} fusion(bf16[1024,768]{1,0:T(8,128)(2,1)} %param.5, f32[768]{0:T(1024)} %param.6, f32[1024]{0:T(1024)S(1)} %get-tuple-element.11), kind=kLoop, calls=%fused_computation.11 | loop fusion | flops 53477376 | bytes 3152896 | tf_op jit(solution)/shard_map/convert_element_type | solution.py:31
  17.9 2.2 collective-permute-start.1
  20.1 1.5 collective-permute-start
  21.6 7.8 %fusion.80 = bf16[1,1024,768]{2,1,0:T(8,128)(2,1)S(1)} fusion(f32[768]{0:T(1024)S(1)} %copy-done.7, f32[1024]{0:T(1024)S(1)} %get-tuple-element.11, bf16[1024,768]{1,0:T(8,128)(2,1)S(1)} %copy-done.1), kind=kLoop, calls=%fused_computation.97 | loop fusion | flops 53477376 | bytes 3152896 | tf_op jit(solution)/shard_map/stack | solution.py:34
  29.5 57.3 %collective-permute-done.1 = bf16[1024,768]{1,0:T(8,128)(2,1)S(1)} collective-permute-done((bf16[1024,768]{1,0:T(8,128)(2,1)S(1)}, bf16[1024,768]{1,0:T(8,128)(2,1)S(1)}, u32[]{:S(2)}, u32[]{:S(2)}) %collective-permute-start.1) | collective-permute-done | bytes 1572896 | tf_op jit(solution)/shard_map/ppermute | solution.py:14
  86.8 5.7 %fusion.44 = (bf16[1024,384]{1,0:T(8,128)(2,1)S(1)}, f32[1024,384,1]{1,0,2:T(8,128)S(1)}) fusion(bf16[3,768,384]{2,1,0:T(8,128)(2,1)S(1)} %copy-done, bf16[1,1024,768]{2,1,0:T(8,128)(2,1)S(1)} %bitcast.80, bf16[1,1024,768]{2,1,0:T(8,128)(2,1)S(1)} %fusion.80, bf16[1,1024,768]{2,1,0:T(8,128)(2,1)S(1)} %bitcast.82), kind=kOutput, calls=%fused_computation.57 | convolution fusion | flops 1842216960 | bytes 8847360 | tf_op jit(solution)/shard_map/kbc,kch->bh/dot_general | solution.py:35
  92.5 1.8 convolution_multiply_fusion.1
  94.3 1.3 fusion.65
  95.6 6.3 %fusion.69 = (bf16[3,1024,768]{2,1,0:T(8,128)(2,1)S(1)}, f32[3,1024,768]{2,1,0:T(8,128)}) fusion(bf16[1024,384,1]{1,0,2:T(8,128)(2,1)S(1)} %fusion.65, bf16[3,768,384]{2,1,0:T(8,128)(2,1)S(1)} %copy-done), kind=kOutput, calls=%fused_computation.96 | convolution fusion | flops 1814298624 | bytes 16711680 | tf_op jit(solution)/shard_map/bh,kch->kbc/dot_general | solution.py:48
  101.9 1.9 slice_bitcast_fusion.2
  103.8 5.3 %collective-permute-start.2 = (bf16[1024,768]{1,0:T(8,128)(2,1)}, bf16[1024,768]{1,0:T(8,128)(2,1)}, u32[]{:S(2)}, u32[]{:S(2)}) collective-permute-start(bf16[1024,768]{1,0:T(8,128)(2,1)} %get-tuple-element.8), channel_id=1, source_target_pairs={{2,0},{3,1},{4,2},{5,3},{6,4},{7,5},{8,6},{9,7},{10,8},{11,9},{12,... | collective-permute-start | bytes 4718600 | tf_op jit(solution)/shard_map/ppermute | solution.py:14
  109.1 1.5 collective-permute-start.3
  110.6 4.1 %convolution_multiply_fusion = f32[3,768,384]{2,1,0:T(8,128)} fusion(bf16[1024,384,1]{1,0,2:T(8,128)(2,1)S(1)} %fusion.65, bf16[1,1024,768]{2,1,0:T(8,128)(2,1)S(1)} %bitcast.81, bf16[1,1024,768]{2,1,0:T(8,128)(2,1)S(1)} %fusion.80, bf16[1,1024,768]{2,1,0:T(8,128)(2,1)S(1)} %bitcast.83), kind=kOutput, calls=%fused_computation.53 | convolution fusion | flops 1817542656 | bytes 9043968 | tf_op jit(solution)/shard_map/kbc,bh->kch/dot_general | solution.py:45
  114.7 0.0 all-reduce.3.cloned.1.call-update
  114.7 3.4 %fusion.23 = bf16[1024,768]{1,0:T(8,128)(2,1)} fusion(bf16[1024,768]{1,0:T(8,128)(2,1)S(1)} %copy-done.1, bf16[1024,384]{1,0:T(8,128)(2,1)} %copy-done.4, bf16[384,768]{1,0:T(8,128)(2,1)} %param.8), kind=kOutput, calls=%fused_computation.32 | convolution fusion | flops 606339072 | bytes 4521984 | tf_op jit(solution)/shard_map/dot_general | solution.py:38
  118.1 68.6 %collective-permute-done.2 = bf16[1024,768]{1,0:T(8,128)(2,1)} collective-permute-done((bf16[1024,768]{1,0:T(8,128)(2,1)}, bf16[1024,768]{1,0:T(8,128)(2,1)}, u32[]{:S(2)}, u32[]{:S(2)}) %collective-permute-start.2) | collective-permute-done | bytes 1572896 | tf_op jit(solution)/shard_map/ppermute | solution.py:14
  186.7 5.1 %fusion.27 = (f32[1024]{0:T(1024)S(1)}, f32[1024,768]{1,0:T(8,128)S(1)}) fusion(bf16[1024,768]{1,0:T(8,128)(2,1)S(1)} %copy-done.1, f32[768]{0:T(1024)S(1)} %copy-done.7, f32[1024]{0:T(1024)S(1)} %get-tuple-element.11, bf16[1024,768]{1,0:T(8,128)(2,1)} %collective-permute-done.3, bf16[1024,768]{1,0:T(8,128)(2,1)} %collective-permute-done.2, ...), kind=kLoop, calls=%fused_computation.36 | loop fusion | flops 14941184 | bytes 11021312 | tf_op jit(solution)/shard_map/reduce_sum | solution.py:56
  191.9 1.9 fusion.26
  193.8 70.0 %all-reduce.3.cloned.1.call-done = (f32[3,768,384]{2,1,0:T(8,128)}, f32[384,768]{1,0:T(8,128)}) async-done(((f32[3,768,384]{2,1,0:T(8,128)}, f32[384,768]{1,0:T(8,128)}), (f32[3,768,384]{2,1,0:T(8,128)}, f32[384,768]{1,0:T(8,128)})) %all-reduce.3.cloned.1.call-update) | async-done | bytes 4718608 | tf_op jit(solution)/shard_map/psum | solution.py:54
  263.8 4.1 %copy.15 = f32[3,768,384]{2,1,0:T(8,128)} copy(f32[3,768,384]{2,1,0:T(8,128)} %get-tuple-element.18) | data formatting | bytes 7077888
  267.9 1.0 copy.16
  (19 shorter events, 0.1 us)
Async XLA Ops:
  7.2 79.6 %copy-start = (bf16[3,768,384]{2,1,0:T(8,128)(2,1)S(1)}, bf16[3,768,384]{2,1,0:T(8,128)(2,1)}, u32[]{:S(2)}) copy-start(bf16[3,768,384]{2,1,0:T(8,128)(2,1)} %param.7) | copy-start | bytes 5308420
  7.2 14.4 %copy-start.1 = (bf16[1024,768]{1,0:T(8,128)(2,1)S(1)}, bf16[1024,768]{1,0:T(8,128)(2,1)}, u32[]{:S(2)}) copy-start(bf16[1024,768]{1,0:T(8,128)(2,1)} %param.5) | copy-start | bytes 4718596
  7.2 14.4 %copy-start.7 = (f32[768]{0:T(1024)S(1)}, f32[768]{0:T(1024)}, u32[]{:S(2)}) copy-start(f32[768]{0:T(1024)} %param.6) | copy-start | bytes 9220
  7.2 256.6 %all-reduce.3.cloned.1.call-start = ((), (), s32[]{:S(2)}) async-start(), calls=%async_computation | async-start | bytes 9437184 | tf_op jit(solution)/shard_map/psum | solution.py:54
  17.9 68.9 %collective-permute-start.1 = (bf16[1024,768]{1,0:T(8,128)(2,1)S(1)}, bf16[1024,768]{1,0:T(8,128)(2,1)S(1)}, u32[]{:S(2)}, u32[]{:S(2)}) collective-permute-start(bf16[1024,768]{1,0:T(8,128)(2,1)S(1)} %fusion.2), channel_id=1, source_target_pairs={{2,0},{3,1},{4,2},{5,3},{6,4},{7,5},{8,6},{9,7},{10,8},{11,9},{12,... | collective-permute-start | bytes 4718600 | tf_op jit(solution)/shard_map/ppermute | solution.py:14
  20.1 66.7 %collective-permute-start = (bf16[1024,768]{1,0:T(8,128)(2,1)S(1)}, bf16[1024,768]{1,0:T(8,128)(2,1)S(1)}, u32[]{:S(2)}, u32[]{:S(2)}) collective-permute-start(bf16[1024,768]{1,0:T(8,128)(2,1)S(1)} %fusion.2), channel_id=1, source_target_pairs={{0,2},{1,3},{2,4},{3,5},{4,6},{5,7},{6,8},{7,9},{8,10},{9,11},{10,... | collective-permute-start | bytes 4718600 | tf_op jit(solution)/shard_map/ppermute | solution.py:14
  86.8 5.7 %copy-start.2 = (bf16[1024,768]{1,0:T(8,128)(2,1)S(1)}, bf16[1024,768]{1,0:T(8,128)(2,1)}, u32[]{:S(2)}) copy-start(bf16[1024,768]{1,0:T(8,128)(2,1)} %param.9) | copy-start | bytes 4718596
  92.5 1.9 copy-start.4
  92.5 1.9 copy-start.6
  103.8 82.9 %collective-permute-start.2 = (bf16[1024,768]{1,0:T(8,128)(2,1)}, bf16[1024,768]{1,0:T(8,128)(2,1)}, u32[]{:S(2)}, u32[]{:S(2)}) collective-permute-start(bf16[1024,768]{1,0:T(8,128)(2,1)} %get-tuple-element.8), channel_id=1, source_target_pairs={{2,0},{3,1},{4,2},{5,3},{6,4},{7,5},{8,6},{9,7},{10,8},{11,9},{12,... | collective-permute-start | bytes 4718600 | tf_op jit(solution)/shard_map/ppermute | solution.py:14
  109.1 77.7 %collective-permute-start.3 = (bf16[1024,768]{1,0:T(8,128)(2,1)}, bf16[1024,768]{1,0:T(8,128)(2,1)}, u32[]{:S(2)}, u32[]{:S(2)}) collective-permute-start(bf16[1024,768]{1,0:T(8,128)(2,1)} %get-tuple-element.9), channel_id=1, source_target_pairs={{0,2},{1,3},{2,4},{3,5},{4,6},{5,7},{6,8},{7,9},{8,10},{9,11},{10,... | collective-permute-start | bytes 4718600 | tf_op jit(solution)/shard_map/ppermute | solution.py:14
  186.7 5.1 %copy-start.3 = (bf16[1024,768]{1,0:T(8,128)(2,1)S(1)}, bf16[1024,768]{1,0:T(8,128)(2,1)}, u32[]{:S(2)}) copy-start(bf16[1024,768]{1,0:T(8,128)(2,1)} %param.9) | copy-start | bytes 4718596
  263.8 4.1 %copy-start.5 = (f32[384,768]{1,0:T(8,128)S(1)}, f32[384,768]{1,0:T(8,128)}, u32[]{:S(2)}) copy-start(f32[384,768]{1,0:T(8,128)} %get-tuple-element.19) | copy-start | bytes 3538948
Sparse Core Ops, SparseCore 0:
  114.8 148.8 all-reduce.2
where the time goes:
time: 279 us; the launch traced here: 276 us
  waiting for transfers between devices  196 us (70%)
  other arithmetic  25.5 us (9%)
  matrix products  22.6 us (8%)
  between operations  14.2 us (5%)
  starting transfers between devices  10.5 us (4%)
  local copies, waits for them, and re-layouts  7.03 us (3%)
    ppermute x4, waiting for transfers between devices, passed_along(): return lax.ppermute(block, axis, route)  126 us
    psum x1, waiting for transfers between devices, shards(): conv_grad, output_grad = lax.psum((conv_term, output_term), 'seq')  70 us
    ppermute x4, starting transfers between devices, passed_along(): return lax.ppermute(block, axis, route)  10.5 us
    convert_element_type x1, other arithmetic, shards(): jax.nn.gelu(normed, approximate=False).astype(jnp.bfloat16)  8.68 us
    another operation x1, other arithmetic, shards(): stacked = jnp.stack([earlier_taps, activated_signal, later_taps])  7.82 us
    dot_general x1, matrix products, shards(): jnp.einsum('bh,kch->kbc', hidden_grad, conv_weight, preferred_element_typ...  6.29 us
    dot_general x1, matrix products, shards(): jnp.einsum('kbc,kch->bh', stacked, conv_weight, preferred_element_type=jn...  5.69 us
  transfers between devices with their start and end apart: 5, of which 3 were waited for; matrix products, arithmetic and copies ran while one was open for 8% of the time, Pallas kernels for 0%

commit v1 on v0

v1 whole, which is shorter than its diff:
```python
import math

import jax
import jax.numpy as jnp
from jax import lax
from jax.sharding import PartitionSpec as P

epsilon = 1e-06


def passed_along(block, axis, distance):
    devices = range(lax.axis_size(axis))
    route = [(i - distance, i) for i in devices if i - distance in devices]
    return lax.ppermute(block, axis, route)


def gelu_cdf(value):
    return 0.5 * (1.0 + jax.scipy.special.erf(value * (1.0 / math.sqrt(2.0))))


def gelu_slope(value, cdf):
    return cdf + value * jnp.exp(-0.5 * value * value) * (1.0 / math.sqrt(2.0 * math.pi))


def dot(left, right, contract):
    return lax.dot_general(left, right, (contract, ((), ())), preferred_element_type=jnp.float32)


def shards(signal, norm_gain, conv_weight, output_weight, cotangent):
    devices = lax.axis_size("seq")
    stride = devices // 8
    local_bins = signal.shape[0]
    odd = (lax.axis_index("seq") // stride) % 2 == 1
    far_weight = jnp.where(odd, conv_weight[0], conv_weight[2])
    near_weight = jnp.where(odd, conv_weight[2], conv_weight[0])
    far_route, near_route = [], []
    for i in range(devices):
        is_odd = (i // stride) % 2 == 1
        target = i + 2 * stride if is_odd else i - 2 * stride
        if 0 <= target < devices:
            far_route.append((i, target))
        near_route.append((i, i - stride if is_odd else i + stride))

    signal_f = signal.astype(jnp.float32)
    mean_square = jnp.mean(signal_f * signal_f, axis=-1, keepdims=True)
    inverse_rms = lax.rsqrt(mean_square + epsilon)
    normed = signal_f * inverse_rms * norm_gain
    normed_cdf = gelu_cdf(normed)
    activated = (normed * normed_cdf).astype(jnp.bfloat16)

    chunks = 2
    rows = local_bins // chunks
    parts = []
    for j in range(chunks):
        block = activated[j * rows : (j + 1) * rows]
        far = dot(block, far_weight, ((1,), (0,))).astype(jnp.bfloat16)
        parts.append(lax.ppermute(far, "seq", far_route))
    arrived = []
    for j in range(chunks):
        block = activated[j * rows : (j + 1) * rows]
        near = dot(block, near_weight, ((1,), (0,))) + parts[j].astype(jnp.float32)
        arrived.append(lax.ppermute(near.astype(jnp.bfloat16), "seq", near_route))
    hidden = dot(activated, conv_weight[1], ((1,), (0,))) + jnp.concatenate(arrived).astype(
        jnp.float32
    )
    hidden_cdf = gelu_cdf(hidden)
    gated = (hidden * hidden_cdf).astype(jnp.bfloat16)
    gated_grad = dot(cotangent, output_weight, ((1,), (1,)))
    hidden_grad = (gated_grad * gelu_slope(hidden, hidden_cdf)).astype(jnp.bfloat16)
    earlier = passed_along(hidden_grad, "seq", stride)
    later = passed_along(hidden_grad, "seq", -stride)

    grad_scale = 1.0 / math.sqrt(local_bins * devices)
    block_out = (signal_f + dot(gated, output_weight, ((1,), (0,)))).astype(jnp.bfloat16)
    output_term = dot(gated, cotangent, ((0,), (0,))) * grad_scale
    middle_term = dot(activated, hidden_grad, ((0,), (0,))) * grad_scale
    output_grad, middle_grad = lax.psum((output_term, middle_term), "seq")
    first_term = dot(activated, later, ((0,), (0,))) * grad_scale
    last_term = dot(activated, earlier, ((0,), (0,))) * grad_scale
    first_grad, last_grad = lax.psum((first_term, last_term), "seq")
    conv_grad = jnp.stack([first_grad, middle_grad, last_grad])

    input_gradient = (
        dot(hidden_grad, conv_weight[1], ((1,), (1,)))
        + dot(later, conv_weight[0], ((1,), (1,)))
        + dot(earlier, conv_weight[2], ((1,), (1,)))
    )
    weighted = input_gradient * gelu_slope(normed, normed_cdf) * norm_gain
    inner = jnp.mean(weighted * signal_f, axis=-1, keepdims=True)
    cubed = inverse_rms * inverse_rms * inverse_rms
    signal_grad = cotangent.astype(jnp.float32) + weighted * inverse_rms - signal_f * cubed * inner
    return (block_out, signal_grad.astype(jnp.bfloat16), conv_grad, output_grad)


def solution(mesh):
    placed = (P(("groups", "seq"), None), P(), P(), P(), P(("groups", "seq"), None))
    return jax.shard_map(
        shards,
        mesh=mesh,
        in_specs=placed,
        out_specs=(
            P(("groups", "seq"), None),
            P(("groups", "seq"), None),
            P("groups", None, None),
            P("groups", None),
        ),
        check_vma=False,
    )
```

time: 279 us -> 219 us (0.78)
  waiting for transfers between devices: 196 us -> 162 us
  other arithmetic: 25.5 us -> 9.28 us
  local copies, waits for them, and re-layouts: 7.03 us -> 2.39 us
  matrix products: 22.6 us -> 19.4 us
    ppermute x4 -> x2, waiting for transfers between devices: 126 us -> 25.7 us  [passed_along(): return lax.ppermute(block, axis, route)]
    psum x1, waiting for transfers between devices: 70 us -> 111 us  [shards(): first_grad, last_grad = lax.psum((first_term, last_term), 'seq')]
    ppermute x0 -> x4, waiting for transfers between devices: none -> 25.5 us  [the longest x2 16.4 us: shards(): parts.append(lax.ppermute(far, 'seq', far_route))]
    convert_element_type x1, other arithmetic: 8.68 us -> 1.33 us  [shards(): activated = (normed * normed_cdf).astype(jnp.bfloat16)]
    reduce_sum x1 -> x0, other arithmetic: 5.1 us -> none  [shards(): inner = jnp.mean(weighted * signal_f, axis=-1, keepdims=True)]
    ppermute x4 -> x2, starting transfers between devices: 10.5 us -> 5.51 us  [passed_along(): return lax.ppermute(block, axis, route)]
    another operation x1, other arithmetic: 7.82 us -> 4.1 us  [shards(): conv_grad = jnp.stack([first_grad, middle_grad, last_grad])]
    dot_general x6 -> x14, matrix products: 22.6 us -> 19.4 us  [dot(): lax.dot_general(left, right, (contract, ((), ())), preferred_element_type...]
  transfers between devices with their start and end apart: 5 -> 7, of which waited for: 3 -> 6; matrix products, arithmetic and copies ran while one was open for 8% -> 8% of each run, Pallas kernels for 0% -> 0%
where the time goes in v1:
time: 219 us; the launch traced here: 216 us
  waiting for transfers between devices  162 us (74%)
  matrix products  19.4 us (9%)
  between operations  14.3 us (7%)
  other arithmetic  9.28 us (4%)
  starting transfers between devices  8.27 us (4%)
  local copies, waits for them, and re-layouts  2.39 us (1%)
    psum x1, waiting for transfers between devices, shards(): first_grad, last_grad = lax.psum((first_term, last_term), 'seq')  111 us
    ppermute x2, waiting for transfers between devices, passed_along(): return lax.ppermute(block, axis, route)  25.7 us
    dot_general x14, matrix products, dot(): lax.dot_general(left, right, (contract, ((), ())), preferred_element_type...  19.4 us
    ppermute x2, waiting for transfers between devices, shards(): parts.append(lax.ppermute(far, 'seq', far_route))  16.4 us
    ppermute x2, waiting for transfers between devices, shards(): arrived.append(lax.ppermute(near.astype(jnp.bfloat16), 'seq', near_route))  9.03 us
    ppermute x2, starting transfers between devices, passed_along(): return lax.ppermute(block, axis, route)  5.51 us
  transfers between devices with their start and end apart: 7, of which 6 were waited for; matrix products, arithmetic and copies ran while one was open for 8% of the time, Pallas kernels for 0%

profile of v1, /device:TPU:31, one launch (start us, length us, event | category | flops | bytes accessed | tf_op | source)
XLA Modules:
  0.0 216.0 jit_solution(4862582799445642327)
XLA Ops:
  7.3 1.9 fusion.6
  9.3 1.3 fusion.13
  11.3 1.3 collective-permute-start.2
  13.2 1.3 collective-permute-start
  14.5 8.7 %collective-permute-done.2 = bf16[512,384]{1,0:T(8,128)(2,1)S(1)} collective-permute-done((bf16[512,384]{1,0:T(8,128)(2,1)S(1)}, bf16[512,384]{1,0:T(8,128)(2,1)S(1)}, u32[]{:S(2)}, u32[]{:S(2)}) %collective-permute-start.2) | collective-permute-done | bytes 393248 | tf_op jit(solution)/shard_map/ppermute | solution.py:57
  23.8 7.8 %collective-permute-done = bf16[512,384]{1,0:T(8,128)(2,1)S(1)} collective-permute-done((bf16[512,384]{1,0:T(8,128)(2,1)S(1)}, bf16[512,384]{1,0:T(8,128)(2,1)S(1)}, u32[]{:S(2)}, u32[]{:S(2)}) %collective-permute-start) | collective-permute-done | bytes 393248 | tf_op jit(solution)/shard_map/ppermute | solution.py:57
  32.3 9.0 %collective-permute-done.1 = bf16[512,384]{1,0:T(8,128)(2,1)S(1)} collective-permute-done((bf16[512,384]{1,0:T(8,128)(2,1)S(1)}, bf16[512,384]{1,0:T(8,128)(2,1)S(1)}, u32[]{:S(2)}, u32[]{:S(2)}) %collective-permute-start.1) | collective-permute-done | bytes 393248 | tf_op jit(solution)/shard_map/ppermute | solution.py:62
  41.3 1.1 multiply_convert_fusion
  42.5 1.3 fusion.24
  43.8 1.3 collective-permute-start.5
  45.1 4.2 %collective-permute-start.4 = (bf16[1024,384]{1,0:T(8,128)(2,1)S(1)}, bf16[1024,384]{1,0:T(8,128)(2,1)S(1)}, u32[]{:S(2)}, u32[]{:S(2)}) collective-permute-start(bf16[1024,384]{1,0:T(8,128)(2,1)S(1)} %fusion.24), channel_id=1, source_target_pairs={{2,0},{3,1},{4,2},{5,3},{6,4},{7,5},{8,6},{9,7},{10,8},{11,9},{12,... | collective-permute-start | bytes 2359304 | tf_op jit(solution)/shard_map/ppermute | solution.py:14
  49.3 2.0 fusion.26
  51.3 1.9 convolution_multiply_fusion
  53.2 9.0 %collective-permute-done.5 = bf16[1024,384]{1,0:T(8,128)(2,1)S(1)} collective-permute-done((bf16[1024,384]{1,0:T(8,128)(2,1)S(1)}, bf16[1024,384]{1,0:T(8,128)(2,1)S(1)}, u32[]{:S(2)}, u32[]{:S(2)}) %collective-permute-start.5) | collective-permute-done | bytes 786464 | tf_op jit(solution)/shard_map/ppermute | solution.py:14
  62.2 2.0 fusion.25
  64.3 16.7 %collective-permute-done.4 = bf16[1024,384]{1,0:T(8,128)(2,1)S(1)} collective-permute-done((bf16[1024,384]{1,0:T(8,128)(2,1)S(1)}, bf16[1024,384]{1,0:T(8,128)(2,1)S(1)}, u32[]{:S(2)}, u32[]{:S(2)}) %collective-permute-start.4) | collective-permute-done | bytes 786464 | tf_op jit(solution)/shard_map/ppermute | solution.py:14
  81.9 2.1 fusion.27
  84.0 2.1 fusion.14
  87.3 1.0 fusion.38
  88.4 2.5 %fusion.18 = (f32[1024]{0:T(1024)S(1)}, f32[1024,768]{1,0:T(8,128)S(1)}) fusion(bf16[1024,768]{1,0:T(8,128)(2,1)S(1)} %copy-done.1, f32[768]{0:T(1024)S(1)} %copy-done.11, f32[1024]{0:T(1024)S(1)} %get-tuple-element.9, bf16[1024,384]{1,0:T(8,128)(2,1)S(1)} %copy-done.13, bf16[3,768,384]{2,1,0:T(8,128)(2,1)S(1)} %copy-done.6, f32[1024,768]{1,0:T(8,128)S(1)} %fusion.41, ...), kind=kOutput, calls=%fused_computation.25 | convolution fusion | flops 617348096 | bytes 12398592 | tf_op jit(solution)/shard_map/dot_general | solution.py:26
  91.0 1.9 fusion.17
  92.9 111.1 %all-reduce.3.cloned.1.call-done = (f32[1,768,384]{2,1,0:T(8,128)}, f32[1,768,384]{2,1,0:T(8,128)}, f32[1,768,384]{2,1,0:T(8,128)}, f32[384,768]{1,0:T(8,128)}) async-done(((f32[1,768,384]{2,1,0:T(8,128)}, f32[1,768,384]{2,1,0:T(8,128)}, f32[1,768,384]{2,1,0:T(8,128)}, f32[384,768]{1,0:T(8,128)}), (f32[1,768,384]{2,1,0:T(8,128)}, f32[1,768,384]{2,1,0:T(8,128)}, f32[1,768,384]{2,1,0:T(8,128)}, ...) | async-done | bytes 4718608 | tf_op jit(solution)/shard_map/psum | solution.py:80
  204.0 4.1 %pad_maximum_fusion = f32[3,768,384]{2,1,0:T(8,128)} fusion(f32[1,768,384]{2,1,0:T(8,128)} %get-tuple-element.4, f32[1,768,384]{2,1,0:T(8,128)} %get-tuple-element.5, f32[1,768,384]{2,1,0:T(8,128)} %get-tuple-element.6), kind=kLoop, calls=%fused_computation.6 | loop fusion | flops 1769472 | bytes 7077888 | tf_op jit(solution)/shard_map/stack | solution.py:81
  208.1 1.0 copy.19
  (40 shorter events, 4.9 us)
Async XLA Ops:
  7.2 35.3 %copy-start = (bf16[384,768]{1,0:T(8,128)(2,1)S(1)}, bf16[384,768]{1,0:T(8,128)(2,1)}, u32[]{:S(2)}) copy-start(bf16[384,768]{1,0:T(8,128)(2,1)} %param.8) | copy-start | bytes 1769476
  7.2 2.0 copy-start.1
  7.2 2.0 copy-start.11
  7.2 196.8 %all-reduce.3.cloned.1.call-start = ((), (), s32[]{:S(2)}) async-start(), calls=%async_computation | async-start | bytes 9437184 | tf_op jit(solution)/shard_map/psum | solution.py:80
  9.2 1.5 copy-start.5
  11.3 11.9 %collective-permute-start.2 = (bf16[512,384]{1,0:T(8,128)(2,1)S(1)}, bf16[512,384]{1,0:T(8,128)(2,1)S(1)}, u32[]{:S(2)}, u32[]{:S(2)}) collective-permute-start(bf16[512,384]{1,0:T(8,128)(2,1)S(1)} %convolution_convert_fusion), channel_id=1, source_target_pairs={{2,6},{3,7},{4,0},{5,1},{6,10},{7,11},{8,4},{9,5},{10,14},{11,15},... | collective-permute-start | bytes 1179656 | tf_op jit(solution)/shard_map/ppermute | solution.py:57
  13.2 18.4 %collective-permute-start = (bf16[512,384]{1,0:T(8,128)(2,1)S(1)}, bf16[512,384]{1,0:T(8,128)(2,1)S(1)}, u32[]{:S(2)}, u32[]{:S(2)}) collective-permute-start(bf16[512,384]{1,0:T(8,128)(2,1)S(1)} %convolution_convert_fusion.1), channel_id=1, source_target_pairs={{2,6},{3,7},{4,0},{5,1},{6,10},{7,11},{8,4},{9,5},{10,14},{11,15},... | collective-permute-start | bytes 1179656 | tf_op jit(solution)/shard_map/ppermute | solution.py:57
  23.7 8.5 %collective-permute-start.3 = (bf16[512,384]{1,0:T(8,128)(2,1)S(1)}, bf16[512,384]{1,0:T(8,128)(2,1)S(1)}, u32[]{:S(2)}, u32[]{:S(2)}) collective-permute-start(bf16[512,384]{1,0:T(8,128)(2,1)S(1)} %add_convert_fusion), channel_id=1, source_target_pairs={{0,2},{1,3},{2,0},{3,1},{4,6},{5,7},{6,4},{7,5},{8,10},{9,11},{10,... | collective-permute-start | bytes 1179656 | tf_op jit(solution)/shard_map/ppermute | solution.py:62
  32.2 10.3 %copy-start.2 = (bf16[1024,768]{1,0:T(8,128)(2,1)S(1)}, bf16[1024,768]{1,0:T(8,128)(2,1)}, u32[]{:S(2)}) copy-start(bf16[1024,768]{1,0:T(8,128)(2,1)} %param.9) | copy-start | bytes 4718596
  32.2 9.1 %collective-permute-start.1 = (bf16[512,384]{1,0:T(8,128)(2,1)S(1)}, bf16[512,384]{1,0:T(8,128)(2,1)S(1)}, u32[]{:S(2)}, u32[]{:S(2)}) collective-permute-start(bf16[512,384]{1,0:T(8,128)(2,1)S(1)} %add_convert_fusion.1), channel_id=1, source_target_pairs={{0,2},{1,3},{2,0},{3,1},{4,6},{5,7},{6,4},{7,5},{8,10},{9,11},{10,... | collective-permute-start | bytes 1179656 | tf_op jit(solution)/shard_map/ppermute | solution.py:62
  43.8 7.6 %copy-start.7 = (bf16[1024,384]{1,0:T(8,128)(2,1)}, bf16[1024,384]{1,0:T(8,128)(2,1)S(1)}, u32[]{:S(2)}) copy-start(bf16[1024,384]{1,0:T(8,128)(2,1)S(1)} %fusion.24) | copy-start | bytes 2359300
  43.8 18.4 %collective-permute-start.5 = (bf16[1024,384]{1,0:T(8,128)(2,1)S(1)}, bf16[1024,384]{1,0:T(8,128)(2,1)S(1)}, u32[]{:S(2)}, u32[]{:S(2)}) collective-permute-start(bf16[1024,384]{1,0:T(8,128)(2,1)S(1)} %fusion.24), channel_id=1, source_target_pairs={{0,2},{1,3},{2,4},{3,5},{4,6},{5,7},{6,8},{7,9},{8,10},{9,11},{10,... | collective-permute-start | bytes 2359304 | tf_op jit(solution)/shard_map/ppermute | solution.py:14
  45.1 35.9 %collective-permute-start.4 = (bf16[1024,384]{1,0:T(8,128)(2,1)S(1)}, bf16[1024,384]{1,0:T(8,128)(2,1)S(1)}, u32[]{:S(2)}, u32[]{:S(2)}) collective-permute-start(bf16[1024,384]{1,0:T(8,128)(2,1)S(1)} %fusion.24), channel_id=1, source_target_pairs={{2,0},{3,1},{4,2},{5,3},{6,4},{7,5},{8,6},{9,7},{10,8},{11,9},{12,... | collective-permute-start | bytes 2359304 | tf_op jit(solution)/shard_map/ppermute | solution.py:14
  62.2 2.0 copy-start.12
  81.0 0.9 copy-start.9
  84.0 2.1 copy-start.6
  84.0 2.1 copy-start.8
  86.1 1.1 copy-start.10
  87.3 1.1 copy-start.13
  88.4 2.5 %copy-start.3 = (bf16[1024,768]{1,0:T(8,128)(2,1)S(1)}, bf16[1024,768]{1,0:T(8,128)(2,1)}, u32[]{:S(2)}) copy-start(bf16[1024,768]{1,0:T(8,128)(2,1)} %param.9) | copy-start | bytes 4718596
  204.0 4.1 %copy-start.4 = (f32[384,768]{1,0:T(8,128)S(1)}, f32[384,768]{1,0:T(8,128)}, u32[]{:S(2)}) copy-start(f32[384,768]{1,0:T(8,128)} %get-tuple-element.17) | copy-start | bytes 3538948
Sparse Core Ops, SparseCore 0:
  84.1 119.8 all-reduce.2

commit v2 on v1

--- a/solution.py
+++ b/solution.py
@@ -1,8 +1,11 @@
+import functools
 import math
 
 import jax
 import jax.numpy as jnp
 from jax import lax
+from jax.experimental import pallas as pl
+from jax.experimental.pallas import tpu as pltpu
 from jax.sharding import PartitionSpec as P
 
 epsilon = 1e-06
@@ -24,6 +27,203 @@
 
 def dot(left, right, contract):
     return lax.dot_general(left, right, (contract, ((), ())), preferred_element_type=jnp.float32)
+
+
+def backward(
+    devices, signal, cotangent, activated, hidden_grad, gated, conv_weight, norm_gain,
+    signal_grad, grads,
+    earlier, later, mine, from_sibling, half, pieces,
+    halo_send, halo_recv, pair_send, pair_recv, scatter_send, scatter_recv,
+    gather_send, gather_recv, back_send, back_recv,
+):
+    stride = devices // 8
+    chips = devices // 2
+    channels, width = conv_weight.shape[1:]
+    bins = signal.shape[0]
+    piece = channels // chips
+    me = lax.axis_index("seq")
+    chip, core = me // 2, me % 2
+    sibling = chip * 2 + 1 - core
+
+    def peer(distance):
+        other = lax.rem(chip + distance, chips)
+        return other, {"seq": other * 2 + core}
+
+    barrier = pltpu.get_barrier_semaphore()
+    pl.semaphore_signal(barrier, inc=1, device_id={"seq": sibling})
+    for distance in range(1, chips):
+        pl.semaphore_signal(barrier, inc=1, device_id=peer(distance)[1])
+    pl.semaphore_wait(barrier, chips)
+
+    has_after, has_before = me + stride < devices, me >= stride
+    to_after = pltpu.make_async_remote_copy(
+        hidden_grad, earlier, halo_send.at[0], halo_recv.at[0],
+        device_id={"seq": lax.rem(me + stride, devices)},
+    )
+    to_before = pltpu.make_async_remote_copy(
+        hidden_grad, later, halo_send.at[1], halo_recv.at[1],
+        device_id={"seq": lax.rem(me + devices - stride, devices)},
+    )
+    pl.when(has_after)(to_after.start)
+    pl.when(has_before)(to_before.start)
+
+    @pl.when(jnp.logical_not(has_before))
+    def _():
+        earlier[...] = jnp.zeros_like(earlier)
+
+    @pl.when(jnp.logical_not(has_after))
+    def _():
+        later[...] = jnp.zeros_like(later)
+
+    tile = 256
+
+    def contribution(part, left, right):
+        @pl.loop(0, channels // tile)
+        def _(step):
+            at = pl.ds(pl.multiple_of(step * tile, tile), tile)
+            mine[part, at, :] = dot(left[:, at], right[...], ((0,), (0,))).astype(jnp.bfloat16)
+
+    def start_pair(batch):
+        copy = pltpu.make_async_remote_copy(
+            mine.at[2 * batch + 1 - core], from_sibling.at[batch],
+            pair_send.at[batch], pair_recv.at[batch], device_id={"seq": sibling},
+        )
+        copy.start()
+        return copy
+
+    def start_scatter(batch):
+        half[batch] = (
+            mine[2 * batch + core].astype(jnp.float32) + from_sibling[batch].astype(jnp.float32)
+        ).astype(jnp.bfloat16)
+        copies = []
+        for distance in range(1, chips):
+            other, device = peer(distance)
+            copy = pltpu.make_async_remote_copy(
+                half.at[batch, pl.ds(pl.multiple_of(other * piece, piece), piece)],
+                pieces.at[batch, distance - 1],
+                scatter_send.at[batch, distance - 1], scatter_recv.at[batch, distance - 1],
+                device_id=device,
+            )
+            copy.start()
+            copies.append(copy)
+        return copies
+
+    def start_gather(batch):
+        at = pl.ds(pl.multiple_of(chip * piece, piece), piece)
+        total = half[batch, at, :].astype(jnp.float32)
+        for distance in range(1, chips):
+            total = total + pieces[batch, distance - 1].astype(jnp.float32)
+        grads[2 * batch + core, at, :] = total.astype(jnp.bfloat16)
+        copies = []
+        for distance in range(1, chips):
+            copy = pltpu.make_async_remote_copy(
+                grads.at[2 * batch + core, at], grads.at[2 * batch + core, at],
+                gather_send.at[batch, distance - 1], gather_recv.at[batch, distance - 1],
+                device_id=peer(distance)[1],
+            )
+            copy.start()
+            copies.append(copy)
+        return copies
+
+    def start_back(batch):
+        copy = pltpu.make_async_remote_copy(
+            grads.at[2 * batch + core], grads.at[2 * batch + core],
+            back_send.at[batch], back_recv.at[batch], device_id={"seq": sibling},
+        )
+        copy.start()
+        return copy
+
+    contribution(0, cotangent, gated)
+    contribution(1, activated, hidden_grad)
+    pair0 = start_pair(0)
+    pair0.wait_recv()
+    scatter0 = start_scatter(0)
+
+    pl.when(has_after)(to_before.wait_recv)
+    pl.when(has_before)(to_after.wait_recv)
+    contribution(2, activated, later)
+    contribution(3, activated, earlier)
+    pair1 = start_pair(1)
+    for copy in scatter0:
+        copy.wait_recv()
+    gather0 = start_gather(0)
+    pair1.wait_recv()
+    scatter1 = start_scatter(1)
+
+    @pl.loop(0, bins // tile)
+    def _(step):
+        at = pl.ds(pl.multiple_of(step * tile, tile), tile)
+        signal_f = signal[at, :].astype(jnp.float32)
+        mean_square = jnp.mean(signal_f * signal_f, axis=-1, keepdims=True)
+        inverse_rms = lax.rsqrt(mean_square + epsilon)
+        normed = signal_f * inverse_rms * norm_gain[...]
+        input_gradient = (
+            dot(hidden_grad[at, :], conv_weight[1], ((1,), (1,)))
+            + dot(later[at, :], conv_weight[0], ((1,), (1,)))
+            + dot(earlier[at, :], conv_weight[2], ((1,), (1,)))
+        )
+        weighted = input_gradient * gelu_slope(normed, gelu_cdf(normed)) * norm_gain[...]
+        inner = jnp.mean(weighted * signal_f, axis=-1, keepdims=True)
+        cubed = inverse_rms * inverse_rms * inverse_rms
+        signal_grad[at, :] = (
+            cotangent[at, :].astype(jnp.float32)
+            + weighted * inverse_rms
+            - signal_f * cubed * inner
+        ).astype(jnp.bfloat16)
+
+    for copy in gather0:
+        copy.wait_recv()
+    for copy in gather0:
+        copy.wait_send()
+    back0 = start_back(0)
+    for copy in scatter1:
+        copy.wait_recv()
+    gather1 = start_gather(1)
+    for copy in gather1:
+        copy.wait_recv()
+    for copy in gather1:
+        copy.wait_send()
+    back1 = start_back(1)
+    back0.wait_recv()
+    back1.wait_recv()
+    for copy in [pair0, pair1, back0, back1] + scatter0 + scatter1:
+        copy.wait_send()
+    pl.when(has_after)(to_after.wait_send)
+    pl.when(has_before)(to_before.wait_send)
+
+
+def run_backward(signal, cotangent, activated, hidden_grad, gated, conv_weight, norm_gain):
+    devices = lax.axis_size("seq")
+    chips = devices // 2
+    bins, channels = signal.shape
+    width = hidden_grad.shape[1]
+    bf16 = jnp.bfloat16
+    vmem = pl.BlockSpec(memory_space=pltpu.VMEM)
+    dma = pltpu.SemaphoreType.DMA
+    return pl.pallas_call(
+        functools.partial(backward, devices),
+        out_shape=(
+            jax.ShapeDtypeStruct((bins, channels), bf16),
+            jax.ShapeDtypeStruct((4, channels, width), bf16),
+        ),
+        in_specs=[vmem] * 7,
+        out_specs=(vmem, vmem),
+        scratch_shapes=[
+            pltpu.VMEM((bins, width), bf16),
+            pltpu.VMEM((bins, width), bf16),
+            pltpu.VMEM((4, channels, width), bf16),
+            pltpu.VMEM((2, channels, width), bf16),
+            pltpu.VMEM((2, channels, width), bf16),
+            pltpu.VMEM((2, chips - 1, channels // chips, width), bf16),
+            dma((2,)), dma((2,)), dma((2,)), dma((2,)),
+            dma((2, chips - 1)), dma((2, chips - 1)), dma((2, chips - 1)), dma((2, chips - 1)),
+            dma((2,)), dma((2,)),
+        ],
+        compiler_params=pltpu.CompilerParams(
+            collective_id=0, has_side_effects=True, vmem_limit_bytes=48 << 20
+        ),
+        name="backward",
+    )(signal, cotangent, activated, hidden_grad, gated, conv_weight, norm_gain.reshape(1, -1))
 
 
 def shards(signal, norm_gain, conv_weight, output_weight, cotangent):
@@ -67,6 +267,15 @@
     gated = (hidden * hidden_cdf).astype(jnp.bfloat16)
     gated_grad = dot(cotangent, output_weight, ((1,), (1,)))
     hidden_grad = (gated_grad * gelu_slope(hidden, hidden_cdf)).astype(jnp.bfloat16)
+    if (signal.shape[1] * 2 // devices) % 16 == 0:
+        block_out = (signal_f + dot(gated, output_weight, ((1,), (0,)))).astype(jnp.bfloat16)
+        signal_grad, grads = run_backward(
+            signal, cotangent, activated, hidden_grad, gated, conv_weight, norm_gain
+        )
+        grads = grads.astype(jnp.float32) * (1.0 / math.sqrt(local_bins * devices))
+        conv_grad = jnp.stack([grads[2], grads[1], grads[3]])
+        return block_out, signal_grad, conv_grad, grads[0].T
+
     earlier = passed_along(hidden_grad, "seq", stride)
     later = passed_along(hidden_grad, "seq", -stride)
 

time: 219 us -> 147 us (0.67); the launches traced: 216 us -> 147 us
  waiting for transfers between devices: 162 us -> 25.5 us
  Pallas kernels: 0 us -> 95.8 us
  between operations: 14.3 us -> 0.87 us
  matrix products: 19.4 us -> 6.92 us
  starting transfers between devices: 8.27 us -> 2.73 us
  local copies, waits for them, and re-layouts: 2.39 us -> 5.72 us
    psum x1 -> x0, waiting for transfers between devices: 111 us -> none  [shards(): first_grad, last_grad = lax.psum((first_term, last_term), 'seq')]
    pallas_call x0 -> x1, Pallas kernels: none -> 95.8 us  [run_backward(): pl.pallas_call(functools.partial(backward, devices), out_shape=(jax.Shape...]
    ppermute x2 -> x0, waiting for transfers between devices: 25.7 us -> none  [passed_along(): return lax.ppermute(block, axis, route)]
    dot_general x14 -> x7, matrix products: 19.4 us -> 6.92 us  [dot(): lax.dot_general(left, right, (contract, ((), ())), preferred_element_type...]
    ppermute x2 -> x0, starting transfers between devices: 5.51 us -> none  [passed_along(): return lax.ppermute(block, axis, route)]
    mul x1, other arithmetic: 0.01 us -> 2.54 us  [shards(): grads = grads.astype(jnp.float32) * (1.0 / math.sqrt(local_bins * devices))]
  transfers between devices with their start and end apart: 7 -> 4, of which waited for: 6 -> 3; matrix products, arithmetic and copies ran while one was open for 8% -> 1% of each run, Pallas kernels for 0% -> 0%
where the time goes in v2:
time: 147 us
  Pallas kernels  95.8 us (65%)
  waiting for transfers between devices  25.5 us (17%)
  other arithmetic  9.21 us (6%)
  matrix products  6.92 us (5%)
  local copies, waits for them, and re-layouts  5.72 us (4%)
  starting transfers between devices  2.73 us (2%)
    pallas_call x1, Pallas kernels, run_backward(): pl.pallas_call(functools.partial(backward, devices), out_shape=(jax.Shape...  95.8 us
    ppermute x2, waiting for transfers between devices, shards(): parts.append(lax.ppermute(far, 'seq', far_route))  16.4 us
    ppermute x2, waiting for transfers between devices, shards(): arrived.append(lax.ppermute(near.astype(jnp.bfloat16), 'seq', near_route))  9.03 us
    dot_general x7, matrix products, dot(): lax.dot_general(left, right, (contract, ((), ())), preferred_element_type...  6.92 us
    unnamed x18, local copies, waits for them, and re-layouts  3.97 us
    another operation x1, other arithmetic, shards(): conv_grad = jnp.stack([grads[2], grads[1], grads[3]])  3.41 us
  transfers between devices with their start and end apart: 4, of which 3 were waited for; matrix products, arithmetic and copies ran while one was open for 1% of the time, Pallas kernels for 0%

profile of v2, /device:TPU:31, one launch (start us, length us, event | category | flops | bytes accessed | tf_op | source)
XLA Modules:
  0.0 146.7 jit_solution(9278120258408376011)
XLA Ops:
  0.6 0.0 copy-start
  0.7 1.9 %fusion = f32[1024]{0:T(1024)S(1)} fusion(bf16[1024,768]{1,0:T(8,128)(2,1)} %signal.1), kind=kLoop, calls=%fused_computation.5 | loop fusion | flops 2358272 | bytes 1576960 | tf_op jit(solution)/shard_map/reduce_sum | solution.py:245
  2.7 1.3 fusion.7.activated
  4.0 0.1 copy-done.5
  4.1 0.6 convolution_convert_fusion.1
  4.7 1.3 collective-permute-start
  6.0 0.6 convolution_convert_fusion
  6.6 1.3 collective-permute-start.2
  7.9 8.7 %collective-permute-done = bf16[512,384]{1,0:T(8,128)(2,1)S(1)} collective-permute-done((bf16[512,384]{1,0:T(8,128)(2,1)S(1)}, bf16[512,384]{1,0:T(8,128)(2,1)S(1)}, u32[]{:S(2)}, u32[]{:S(2)}) %collective-permute-start) | collective-permute-done | bytes 393248 | tf_op jit(solution)/shard_map/ppermute | solution.py:257
  16.6 0.6 add_convert_fusion.1
  17.2 0.1 collective-permute-start.1
  17.3 7.7 %collective-permute-done.2 = bf16[512,384]{1,0:T(8,128)(2,1)S(1)} collective-permute-done((bf16[512,384]{1,0:T(8,128)(2,1)S(1)}, bf16[512,384]{1,0:T(8,128)(2,1)S(1)}, u32[]{:S(2)}, u32[]{:S(2)}) %collective-permute-start.2) | collective-permute-done | bytes 393248 | tf_op jit(solution)/shard_map/ppermute | solution.py:257
  25.0 0.6 add_convert_fusion
  25.6 0.1 collective-permute-start.3
  25.7 9.0 %collective-permute-done.3 = bf16[512,384]{1,0:T(8,128)(2,1)S(1)} collective-permute-done((bf16[512,384]{1,0:T(8,128)(2,1)S(1)}, bf16[512,384]{1,0:T(8,128)(2,1)S(1)}, u32[]{:S(2)}, u32[]{:S(2)}) %collective-permute-start.3) | collective-permute-done | bytes 393248 | tf_op jit(solution)/shard_map/ppermute | solution.py:262
  34.8 1.2 multiply_convert_fusion
  35.9 2.1 %fusion.8 = bf16[1024,768]{1,0:T(8,128)(2,1)} fusion(bf16[1024,768]{1,0:T(8,128)(2,1)S(1)} %copy-done.1, bf16[1024,384]{1,0:T(8,128)(2,1)S(1)} %get-tuple-element.16.gated, bf16[384,768]{1,0:T(8,128)(2,1)S(1)} %copy-done), kind=kOutput, calls=%fused_computation.13 | convolution fusion | flops 606339072 | bytes 4521984 | tf_op jit(solution)/shard_map/dot_general | solution.py:29
  38.1 1.3 fusion.14.hidden_grad
  39.4 95.8 %backward.1 = (bf16[1024,768]{1,0:T(8,128)(2,1)S(1)}, bf16[4,768,384]{2,1,0:T(8,128)(2,1)}) custom-call(bf16[1024,768]{1,0:T(8,128)(2,1)S(1)} %copy-done.1, bf16[1024,768]{1,0:T(8,128)(2,1)} %cotangent.1, bf16[1024,768]{1,0:T(8,128)(2,1)} %copy-done.4, bf16[1024,384]{1,0:T(8,128)(2,1)S(1)} %fusion.14.hidden_grad, ...), custom_call_target="tpu_custom_call" | custom-call | tf_op jit(solution)/shard_map/backward/pallas_call | solution.py:203
  135.2 2.5 %convert_multiply_fusion.2 = f32[4,768,384]{2,1,0:T(8,128)S(1)} fusion(bf16[4,768,384]{2,1,0:T(8,128)(2,1)} %get-tuple-element.7), kind=kLoop, calls=%fused_computation.3 | loop fusion | flops 2359296 | bytes 7077888 | tf_op jit(solution)/shard_map/mul | solution.py:275
  137.7 1.8 %slice_bitcast_fusion = (f32[384,768]{0,1:T(8,128)}, f32[1,768,384]{2,1,0:T(8,128)S(1)}, f32[1,768,384]{2,1,0:T(8,128)S(1)}, f32[1,768,384]{2,1,0:T(8,128)}) fusion(f32[4,768,384]{2,1,0:T(8,128)S(1)} %convert_multiply_fusion.2), kind=kLoop, calls=%fused_computation.26 | loop fusion | bytes 9437184 | tf_op jit(solution)/shard_map/transpose | solution.py:277
  139.5 2.7 %copy.9 = f32[384,768]{1,0:T(8,128)} copy(f32[384,768]{0,1:T(8,128)} %get-tuple-element.12) | data formatting | bytes 2359296
  142.1 3.4 %pad_maximum_fusion = f32[3,768,384]{2,1,0:T(8,128)} fusion(f32[1,768,384]{2,1,0:T(8,128)S(1)} %get-tuple-element.13, f32[1,768,384]{2,1,0:T(8,128)S(1)} %get-tuple-element.14, f32[1,768,384]{2,1,0:T(8,128)} %get-tuple-element.15), kind=kLoop, calls=%fused_computation.4 | loop fusion | flops 1769472 | bytes 7077888 | tf_op jit(solution)/shard_map/stack | solution.py:276
  145.6 1.1 copy.11
  (17 shorter events, 0.0 us)
Async XLA Ops:
  0.6 35.3 %copy-start = (bf16[384,768]{1,0:T(8,128)(2,1)S(1)}, bf16[384,768]{1,0:T(8,128)(2,1)}, u32[]{:S(2)}) copy-start(bf16[384,768]{1,0:T(8,128)(2,1)} %param.8) | copy-start | bytes 1769476
  0.6 2.0 %copy-start.1 = (bf16[1024,768]{1,0:T(8,128)(2,1)S(1)}, bf16[1024,768]{1,0:T(8,128)(2,1)}, u32[]{:S(2)}) copy-start(bf16[1024,768]{1,0:T(8,128)(2,1)} %signal.1) | copy-start | bytes 4718596
  0.7 2.0 %copy-start.7 = (f32[768]{0:T(1024)S(1)}, f32[768]{0:T(1024)}, u32[]{:S(2)}) copy-start(f32[768]{0:T(1024)} %param.6) | copy-start | bytes 9220
  2.7 1.5 %copy-start.5 = (bf16[3,768,384]{2,1,0:T(8,128)(2,1)S(1)}, bf16[3,768,384]{2,1,0:T(8,128)(2,1)}, u32[]{:S(2)}) copy-start(bf16[3,768,384]{2,1,0:T(8,128)(2,1)} %conv_weight.1) | copy-start | bytes 5308420
  4.1 30.6 %copy-start.4 = (bf16[1024,768]{1,0:T(8,128)(2,1)}, bf16[1024,768]{1,0:T(8,128)(2,1)S(1)}, u32[]{:S(2)}) copy-start(bf16[1024,768]{1,0:T(8,128)(2,1)S(1)} %fusion.7.activated) | copy-start | bytes 4718596
  4.7 11.9 %collective-permute-start = (bf16[512,384]{1,0:T(8,128)(2,1)S(1)}, bf16[512,384]{1,0:T(8,128)(2,1)S(1)}, u32[]{:S(2)}, u32[]{:S(2)}) collective-permute-start(bf16[512,384]{1,0:T(8,128)(2,1)S(1)} %convolution_convert_fusion.1), channel_id=1, source_target_pairs={{2,6},{3,7},{4,0},{5,1},{6,10},{7,11},{8,4},{9,5},{10,14},{11,15},... | collective-permute-start | bytes 1179656 | tf_op jit(solution)/shard_map/ppermute | solution.py:257
  6.6 18.4 %collective-permute-start.2 = (bf16[512,384]{1,0:T(8,128)(2,1)S(1)}, bf16[512,384]{1,0:T(8,128)(2,1)S(1)}, u32[]{:S(2)}, u32[]{:S(2)}) collective-permute-start(bf16[512,384]{1,0:T(8,128)(2,1)S(1)} %convolution_convert_fusion), channel_id=1, source_target_pairs={{2,6},{3,7},{4,0},{5,1},{6,10},{7,11},{8,4},{9,5},{10,14},{11,15},... | collective-permute-start | bytes 1179656 | tf_op jit(solution)/shard_map/ppermute | solution.py:257
  17.2 8.5 %collective-permute-start.1 = (bf16[512,384]{1,0:T(8,128)(2,1)S(1)}, bf16[512,384]{1,0:T(8,128)(2,1)S(1)}, u32[]{:S(2)}, u32[]{:S(2)}) collective-permute-start(bf16[512,384]{1,0:T(8,128)(2,1)S(1)} %add_convert_fusion.1), channel_id=1, source_target_pairs={{0,2},{1,3},{2,0},{3,1},{4,6},{5,7},{6,4},{7,5},{8,10},{9,11},{10,... | collective-permute-start | bytes 1179656 | tf_op jit(solution)/shard_map/ppermute | solution.py:262
  25.6 9.1 %collective-permute-start.3 = (bf16[512,384]{1,0:T(8,128)(2,1)S(1)}, bf16[512,384]{1,0:T(8,128)(2,1)S(1)}, u32[]{:S(2)}, u32[]{:S(2)}) collective-permute-start(bf16[512,384]{1,0:T(8,128)(2,1)S(1)} %add_convert_fusion), channel_id=1, source_target_pairs={{0,2},{1,3},{2,0},{3,1},{4,6},{5,7},{6,4},{7,5},{8,10},{9,11},{10,... | collective-permute-start | bytes 1179656 | tf_op jit(solution)/shard_map/ppermute | solution.py:262
  35.9 2.1 %copy-start.6 = (bf16[1024,768]{1,0:T(8,128)(2,1)S(1)}, bf16[1024,768]{1,0:T(8,128)(2,1)}, u32[]{:S(2)}) copy-start(bf16[1024,768]{1,0:T(8,128)(2,1)} %cotangent.1) | copy-start | bytes 4718596
  135.2 2.6 %copy-start.2 = (bf16[1024,768]{1,0:T(8,128)(2,1)}, bf16[1024,768]{1,0:T(8,128)(2,1)S(1)}, u32[]{:S(2)}) copy-start(bf16[1024,768]{1,0:T(8,128)(2,1)S(1)} %get-tuple-element.23) | copy-start | bytes 4718596
  142.1 3.4 %copy-start.3 = (bf16[1024,768]{1,0:T(8,128)(2,1)S(1)}, bf16[1024,768]{1,0:T(8,128)(2,1)}, u32[]{:S(2)}) copy-start(bf16[1024,768]{1,0:T(8,128)(2,1)} %copy-done.2) | copy-start | bytes 4718596

commit v3 on v2

--- a/solution.py
+++ b/solution.py
@@ -29,11 +29,14 @@
     return lax.dot_general(left, right, (contract, ((), ())), preferred_element_type=jnp.float32)
 
 
-def backward(
-    devices, signal, cotangent, activated, hidden_grad, gated, conv_weight, norm_gain,
-    signal_grad, grads,
-    earlier, later, mine, from_sibling, half, pieces,
-    halo_send, halo_recv, pair_send, pair_recv, scatter_send, scatter_recv,
+def whole_block(
+    devices, signal, cotangent, conv_weight, output_weight, norm_gain,
+    block_out, signal_grad, grads, output_grad,
+    activated, hidden, gated_grad, gated, hidden_grad,
+    far_out, far_in, near_out, near_in, earlier, later,
+    mine, from_sibling, half, pieces,
+    far_send, far_recv, near_send, near_recv, up_send, up_recv, down_send, down_recv,
+    pair_send, pair_recv, scatter_send, scatter_recv,
     gather_send, gather_recv, back_send, back_recv,
 ):
     stride = devices // 8
@@ -41,13 +44,25 @@
     channels, width = conv_weight.shape[1:]
     bins = signal.shape[0]
     piece = channels // chips
+    grad_scale = 1.0 / math.sqrt(bins * devices)
     me = lax.axis_index("seq")
     chip, core = me // 2, me % 2
     sibling = chip * 2 + 1 - core
+    odd = lax.rem(me // stride, 2)
+    step_sign = 2 * odd - 1
+    far_tap, near_tap = 2 - 2 * odd, 2 * odd
+    tile = 256
+    chunks = bins // tile
+
+    def wrapped(device):
+        return {"seq": lax.rem(device + devices, devices)}
 
     def peer(distance):
         other = lax.rem(chip + distance, chips)
         return other, {"seq": other * 2 + core}
+
+    def rows(step):
+        return pl.ds(pl.multiple_of(step * tile, tile), tile)
 
     barrier = pltpu.get_barrier_semaphore()
     pl.semaphore_signal(barrier, inc=1, device_id={"seq": sibling})
@@ -55,17 +70,39 @@
         pl.semaphore_signal(barrier, inc=1, device_id=peer(distance)[1])
     pl.semaphore_wait(barrier, chips)
 
+    far_target = me + 2 * stride * step_sign
+    far_source = me - 2 * stride * step_sign
+    sends_far = jnp.logical_and(far_target >= 0, far_target < devices)
+    takes_far = jnp.logical_and(far_source >= 0, far_source < devices)
     has_after, has_before = me + stride < devices, me >= stride
-    to_after = pltpu.make_async_remote_copy(
-        hidden_grad, earlier, halo_send.at[0], halo_recv.at[0],
-        device_id={"seq": lax.rem(me + stride, devices)},
-    )
-    to_before = pltpu.make_async_remote_copy(
-        hidden_grad, later, halo_send.at[1], halo_recv.at[1],
-        device_id={"seq": lax.rem(me + devices - stride, devices)},
-    )
-    pl.when(has_after)(to_after.start)
-    pl.when(has_before)(to_before.start)
+
+    def far_copy(step):
+        at = rows(step)
+        return pltpu.make_async_remote_copy(
+            far_out.at[at], far_in.at[at], far_send.at[step], far_recv.at[step],
+            device_id=wrapped(far_target),
+        )
+
+    def near_copy(step):
+        at = rows(step)
+        return pltpu.make_async_remote_copy(
+            near_out.at[at], near_in.at[at], near_send.at[step], near_recv.at[step],
+            device_id=wrapped(me - stride * step_sign),
+        )
+
+    def up_copy(step):
+        at = rows(step)
+        return pltpu.make_async_remote_copy(
+            hidden_grad.at[at], earlier.at[at], up_send.at[step], up_recv.at[step],
+            device_id=wrapped(me + stride),
+        )
+
+    def down_copy(step):
+        at = rows(step)
+        return pltpu.make_async_remote_copy(
+            hidden_grad.at[at], later.at[at], down_send.at[step], down_recv.at[step],
+            device_id=wrapped(me - stride),
+        )
 
     @pl.when(jnp.logical_not(has_before))
     def _():
@@ -75,17 +112,59 @@
     def _():
         later[...] = jnp.zeros_like(later)
 
-    tile = 256
-
-    def contribution(part, left, right):
+    @pl.when(jnp.logical_not(takes_far))
+    def _():
+        far_in[...] = jnp.zeros_like(far_in)
+
+    def normalized(at):
+        signal_f = signal[at, :].astype(jnp.float32)
+        mean_square = jnp.mean(signal_f * signal_f, axis=-1, keepdims=True)
+        inverse_rms = lax.rsqrt(mean_square + epsilon)
+        return signal_f, inverse_rms, signal_f * inverse_rms * norm_gain[...]
+
+    @pl.loop(0, chunks)
+    def _(step):
+        at = rows(step)
+        _, _, normed = normalized(at)
+        block = (normed * gelu_cdf(normed)).astype(jnp.bfloat16)
+        activated[at, :] = block
+        far_out[at, :] = dot(block, conv_weight[far_tap], ((1,), (0,))).astype(jnp.bfloat16)
+        pl.when(sends_far)(far_copy(step).start)
+
+    @pl.loop(0, chunks)
+    def _(step):
+        at = rows(step)
+        pl.when(takes_far)(far_copy(step).wait_recv)
+        block = activated[at, :]
+        near = dot(block, conv_weight[near_tap], ((1,), (0,))) + far_in[at, :].astype(jnp.float32)
+        near_out[at, :] = near.astype(jnp.bfloat16)
+        near_copy(step).start()
+        hidden[at, :] = dot(block, conv_weight[1], ((1,), (0,)))
+        gated_grad[at, :] = dot(cotangent[at, :], output_weight[...], ((1,), (1,)))
+
+    @pl.loop(0, chunks)
+    def _(step):
+        at = rows(step)
+        near_copy(step).wait_recv()
+        value = hidden[at, :] + near_in[at, :].astype(jnp.float32)
+        cdf = gelu_cdf(value)
+        hidden_grad[at, :] = (gated_grad[at, :] * gelu_slope(value, cdf)).astype(jnp.bfloat16)
+        pl.when(has_after)(up_copy(step).start)
+        pl.when(has_before)(down_copy(step).start)
+        gated[at, :] = (value * cdf).astype(jnp.bfloat16)
+
+    def part(batch, side):
+        return 3 - 2 * side if batch == 0 else 2 * side
+
+    def contribution(index, left, right):
         @pl.loop(0, channels // tile)
         def _(step):
-            at = pl.ds(pl.multiple_of(step * tile, tile), tile)
-            mine[part, at, :] = dot(left[:, at], right[...], ((0,), (0,))).astype(jnp.bfloat16)
+            at = rows(step)
+            mine[index, at, :] = dot(left[:, at], right[...], ((0,), (0,))).astype(jnp.bfloat16)
 
     def start_pair(batch):
         copy = pltpu.make_async_remote_copy(
-            mine.at[2 * batch + 1 - core], from_sibling.at[batch],
+            mine.at[part(batch, 1 - core)], from_sibling.at[batch],
             pair_send.at[batch], pair_recv.at[batch], device_id={"seq": sibling},
         )
         copy.start()
@@ -93,7 +172,7 @@
 
     def start_scatter(batch):
         half[batch] = (
-            mine[2 * batch + core].astype(jnp.float32) + from_sibling[batch].astype(jnp.float32)
+            mine[part(batch, core)].astype(jnp.float32) + from_sibling[batch].astype(jnp.float32)
         ).astype(jnp.bfloat16)
         copies = []
         for distance in range(1, chips):
@@ -109,15 +188,16 @@
         return copies
 
     def start_gather(batch):
+        index = part(batch, core)
         at = pl.ds(pl.multiple_of(chip * piece, piece), piece)
         total = half[batch, at, :].astype(jnp.float32)
         for distance in range(1, chips):
             total = total + pieces[batch, distance - 1].astype(jnp.float32)
-        grads[2 * batch + core, at, :] = total.astype(jnp.bfloat16)
+        grads[index, at, :] = total.astype(jnp.bfloat16)
         copies = []
         for distance in range(1, chips):
             copy = pltpu.make_async_remote_copy(
-                grads.at[2 * batch + core, at], grads.at[2 * batch + core, at],
+                grads.at[index, at], grads.at[index, at],
                 gather_send.at[batch, distance - 1], gather_recv.at[batch, distance - 1],
                 device_id=peer(distance)[1],
             )
@@ -126,23 +206,36 @@
         return copies
 
     def start_back(batch):
+        index = part(batch, core)
         copy = pltpu.make_async_remote_copy(
-            grads.at[2 * batch + core], grads.at[2 * batch + core],
+            grads.at[index], grads.at[index],
             back_send.at[batch], back_recv.at[batch], device_id={"seq": sibling},
         )
         copy.start()
         return copy
 
-    contribution(0, cotangent, gated)
+    contribution(3, cotangent, gated)
     contribution(1, activated, hidden_grad)
     pair0 = start_pair(0)
+
+    @pl.loop(0, chunks)
+    def _(step):
+        at = rows(step)
+        block_out[at, :] = (
+            signal[at, :].astype(jnp.float32)
+            + dot(gated[at, :], output_weight[...], ((1,), (0,)))
+        ).astype(jnp.bfloat16)
+
     pair0.wait_recv()
     scatter0 = start_scatter(0)
 
-    pl.when(has_after)(to_before.wait_recv)
-    pl.when(has_before)(to_after.wait_recv)
-    contribution(2, activated, later)
-    contribution(3, activated, earlier)
+    @pl.loop(0, chunks)
+    def _(step):
+        pl.when(has_after)(down_copy(step).wait_recv)
+        pl.when(has_before)(up_copy(step).wait_recv)
+
+    contribution(0, activated, later)
+    contribution(2, activated, earlier)
     pair1 = start_pair(1)
     for copy in scatter0:
         copy.wait_recv()
@@ -150,13 +243,10 @@
     pair1.wait_recv()
     scatter1 = start_scatter(1)
 
-    @pl.loop(0, bins // tile)
-    def _(step):
-        at = pl.ds(pl.multiple_of(step * tile, tile), tile)
-        signal_f = signal[at, :].astype(jnp.float32)
-        mean_square = jnp.mean(signal_f * signal_f, axis=-1, keepdims=True)
-        inverse_rms = lax.rsqrt(mean_square + epsilon)
-        normed = signal_f * inverse_rms * norm_gain[...]
+    @pl.loop(0, chunks)
+    def _(step):
+        at = rows(step)
+        signal_f, inverse_rms, normed = normalized(at)
         input_gradient = (
             dot(hidden_grad[at, :], conv_weight[1], ((1,), (1,)))
             + dot(later[at, :], conv_weight[0], ((1,), (1,)))
@@ -173,63 +263,77 @@
 
     for copy in gather0:
         copy.wait_recv()
-    for copy in gather0:
-        copy.wait_send()
     back0 = start_back(0)
     for copy in scatter1:
         copy.wait_recv()
     gather1 = start_gather(1)
+    back0.wait_recv()
+    output_grad[...] = grads[3].astype(jnp.float32).T * grad_scale
     for copy in gather1:
         copy.wait_recv()
-    for copy in gather1:
+    back1 = start_back(1)
+    back1.wait_recv()
+    for copy in [pair0, pair1, back0, back1] + scatter0 + scatter1 + gather0 + gather1:
         copy.wait_send()
-    back1 = start_back(1)
-    back0.wait_recv()
-    back1.wait_recv()
-    for copy in [pair0, pair1, back0, back1] + scatter0 + scatter1:
-        copy.wait_send()
-    pl.when(has_after)(to_after.wait_send)
-    pl.when(has_before)(to_before.wait_send)
-
-
-def run_backward(signal, cotangent, activated, hidden_grad, gated, conv_weight, norm_gain):
+
+    @pl.loop(0, chunks)
+    def _(step):
+        near_copy(step).wait_send()
+        pl.when(sends_far)(far_copy(step).wait_send)
+        pl.when(has_after)(up_copy(step).wait_send)
+        pl.when(has_before)(down_copy(step).wait_send)
+
+
+def run_whole_block(signal, norm_gain, conv_weight, output_weight, cotangent):
     devices = lax.axis_size("seq")
     chips = devices // 2
     bins, channels = signal.shape
-    width = hidden_grad.shape[1]
-    bf16 = jnp.bfloat16
+    width = output_weight.shape[0]
+    chunks = bins // 256
+    bf16, f32 = jnp.bfloat16, jnp.float32
     vmem = pl.BlockSpec(memory_space=pltpu.VMEM)
     dma = pltpu.SemaphoreType.DMA
+    narrow = pltpu.VMEM((bins, width), bf16)
+    wide = pltpu.VMEM((bins, width), f32)
     return pl.pallas_call(
-        functools.partial(backward, devices),
+        functools.partial(whole_block, devices),
         out_shape=(
             jax.ShapeDtypeStruct((bins, channels), bf16),
+            jax.ShapeDtypeStruct((bins, channels), bf16),
             jax.ShapeDtypeStruct((4, channels, width), bf16),
+            jax.ShapeDtypeStruct((width, channels), f32),
         ),
-        in_specs=[vmem] * 7,
-        out_specs=(vmem, vmem),
+        in_specs=[vmem] * 5,
+        out_specs=(vmem,) * 4,
         scratch_shapes=[
-            pltpu.VMEM((bins, width), bf16),
-            pltpu.VMEM((bins, width), bf16),
+            pltpu.VMEM((bins, channels), bf16), wide, wide, narrow, narrow,
+            narrow, narrow, narrow, narrow, narrow, narrow,
             pltpu.VMEM((4, channels, width), bf16),
             pltpu.VMEM((2, channels, width), bf16),
             pltpu.VMEM((2, channels, width), bf16),
             pltpu.VMEM((2, chips - 1, channels // chips, width), bf16),
-            dma((2,)), dma((2,)), dma((2,)), dma((2,)),
-            dma((2, chips - 1)), dma((2, chips - 1)), dma((2, chips - 1)), dma((2, chips - 1)),
-            dma((2,)), dma((2,)),
-        ],
+        ]
+        + [dma((chunks,))] * 8
+        + [dma((2,))] * 2
+        + [dma((2, chips - 1))] * 4
+        + [dma((2,))] * 2,
         compiler_params=pltpu.CompilerParams(
             collective_id=0, has_side_effects=True, vmem_limit_bytes=48 << 20
         ),
-        name="backward",
-    )(signal, cotangent, activated, hidden_grad, gated, conv_weight, norm_gain.reshape(1, -1))
+        name="whole_block",
+    )(signal, cotangent, conv_weight, output_weight, norm_gain.reshape(1, -1))
 
 
 def shards(signal, norm_gain, conv_weight, output_weight, cotangent):
     devices = lax.axis_size("seq")
     stride = devices // 8
     local_bins = signal.shape[0]
+    if devices == 16:
+        block_out, signal_grad, grads, output_grad = run_whole_block(
+            signal, norm_gain, conv_weight, output_weight, cotangent
+        )
+        conv_grad = grads[:3].astype(jnp.float32) * (1.0 / math.sqrt(local_bins * devices))
+        return block_out, signal_grad, conv_grad, output_grad
     odd = (lax.axis_index("seq") // stride) % 2 == 1
     far_weight = jnp.where(odd, conv_weight[0], conv_weight[2])
     near_weight = jnp.where(odd, conv_weight[2], conv_weight[0])
@@ -267,15 +371,6 @@
     gated = (hidden * hidden_cdf).astype(jnp.bfloat16)
     gated_grad = dot(cotangent, output_weight, ((1,), (1,)))
     hidden_grad = (gated_grad * gelu_slope(hidden, hidden_cdf)).astype(jnp.bfloat16)
-    if (signal.shape[1] * 2 // devices) % 16 == 0:
-        block_out = (signal_f + dot(gated, output_weight, ((1,), (0,)))).astype(jnp.bfloat16)
-        signal_grad, grads = run_backward(
-            signal, cotangent, activated, hidden_grad, gated, conv_weight, norm_gain
-        )
-        grads = grads.astype(jnp.float32) * (1.0 / math.sqrt(local_bins * devices))
-        conv_grad = jnp.stack([grads[2], grads[1], grads[3]])
-        return block_out, signal_grad, conv_grad, grads[0].T
-
     earlier = passed_along(hidden_grad, "seq", stride)
     later = passed_along(hidden_grad, "seq", -stride)
 

time: 147 us -> 126 us (0.86)
  waiting for transfers between devices: 25.5 us -> 0 us
  Pallas kernels: 95.8 us -> 117 us
  matrix products: 6.92 us -> 0 us
  other arithmetic: 9.21 us -> 3.5 us
  starting transfers between devices: 2.73 us -> 0 us
    ppermute x4 -> x0, waiting for transfers between devices: 25.5 us -> none  [the longest x2 16.4 us: shards(): parts.append(lax.ppermute(far, 'seq', far_route))]
    pallas_call x1, Pallas kernels: 95.8 us -> 117 us  [run_whole_block(): pl.pallas_call(functools.partial(whole_block, devices), out_shape=(jax.Sh...]
    dot_general x7 -> x0, matrix products: 6.92 us -> none  [dot(): lax.dot_general(left, right, (contract, ((), ())), preferred_element_type...]
    another operation x1 -> x0, other arithmetic: 3.41 us -> none  [shards(): conv_grad = jnp.stack([grads[2], grads[1], grads[3]])]
    ppermute x4 -> x0, starting transfers between devices: 2.73 us -> none  [the longest x2 2.58 us: shards(): parts.append(lax.ppermute(far, 'seq', far_route))]
    reduce_sum x1 -> x0, other arithmetic: 1.93 us -> none  [shards(): mean_square = jnp.mean(signal_f * signal_f, axis=-1, keepdims=True)]
    transpose x1 -> x0, local copies, waits for them, and re-layouts: 1.75 us -> none  [shards(): return (block_out, signal_grad, conv_grad, grads[0].T)]
    unnamed x18 -> x5, local copies, waits for them, and re-layouts: 3.97 us -> 4.36 us
  transfers between devices with their start and end apart: 4 -> 0, of which waited for: 3 -> 0; matrix products, arithmetic and copies ran while one was open for 1% -> 0% of each run, Pallas kernels for 0% -> 0%
where the time goes in v3:
time: 126 us
  Pallas kernels  117 us (93%)
  local copies, waits for them, and re-layouts  5.05 us (4%)
  other arithmetic  3.5 us (3%)
    pallas_call x1, Pallas kernels, run_whole_block(): pl.pallas_call(functools.partial(whole_block, devices), out_shape=(jax.Sh...  117 us
    unnamed x5, local copies, waits for them, and re-layouts  4.36 us
    mul x1, other arithmetic, shards(): grads[:3].astype(jnp.float32) * (1.0 / math.sqrt(local_bins * devices))  3.5 us

profile of v3, /device:TPU:31, one launch (start us, length us, event | category | flops | bytes accessed | tf_op | source)
XLA Modules:
  0.0 126.2 jit_solution(737659038825395547)
XLA Ops:
  0.6 0.7 reshape.11.norm_gain
  1.3 0.0 copy-start
  1.3 1.1 copy-done
  2.4 117.0 %whole_block.1 = (bf16[1024,768]{1,0:T(8,128)(2,1)S(1)}, bf16[1024,768]{1,0:T(8,128)(2,1)S(1)}, bf16[4,768,384]{2,1,0:T(8,128)(2,1)}, f32[384,768]{1,0:T(8,128)S(1)}) custom-call(bf16[1024,768]{1,0:T(8,128)(2,1)} %signal.1, bf16[1024,768]{1,0:T(8,128)(2,1)} %cotangent.1, bf16[3,768,384]{2,1,0:T(8,128)(2,1)} %conv_weight.1, bf16[384,768]{1,0:T(8,128)(2,1)S(1)} %copy-done, ...), custom_call_target="tpu_custom_call" | custom-call | tf_op jit(solution)/shard_map/whole_block/pallas_call | solution.py:298
  119.4 3.5 %convert_multiply_fusion = f32[3,768,384]{2,1,0:T(8,128)} fusion(bf16[4,768,384]{2,1,0:T(8,128)(2,1)} %get-tuple-element.10), kind=kLoop, calls=%fused_computation | loop fusion | flops 1769472 | bytes 5308416 | tf_op jit(solution)/shard_map/mul | solution.py:335
  122.9 1.1 copy.12
  124.0 1.1 copy.13
  125.2 1.0 copy.14
Async XLA Ops:
  1.3 1.1 copy-start

commit v4 on v3

--- a/solution.py
+++ b/solution.py
@@ -32,7 +32,7 @@
 def whole_block(
     devices, signal, cotangent, conv_weight, output_weight, norm_gain,
     block_out, signal_grad, grads, output_grad,
-    activated, hidden, gated_grad, gated, hidden_grad,
+    activated, transposed, hidden, gated_grad, gated, hidden_grad,
     far_out, far_in, near_out, near_in, earlier, later,
     mine, from_sibling, half, pieces,
     far_send, far_recv, near_send, near_recv, up_send, up_recv, down_send, down_recv,
@@ -51,8 +51,8 @@
     odd = lax.rem(me // stride, 2)
     step_sign = 2 * odd - 1
     far_tap, near_tap = 2 - 2 * odd, 2 * odd
-    tile = 256
-    chunks = bins // tile
+    tile, chunk = 256, 128
+    chunks = bins // chunk
 
     def wrapped(device):
         return {"seq": lax.rem(device + devices, devices)}
@@ -61,8 +61,8 @@
         other = lax.rem(chip + distance, chips)
         return other, {"seq": other * 2 + core}
 
-    def rows(step):
-        return pl.ds(pl.multiple_of(step * tile, tile), tile)
+    def rows(step, size=chunk):
+        return pl.ds(pl.multiple_of(step * size, size), size)
 
     barrier = pltpu.get_barrier_semaphore()
     pl.semaphore_signal(barrier, inc=1, device_id={"seq": sibling})
@@ -130,17 +130,16 @@
         activated[at, :] = block
         far_out[at, :] = dot(block, conv_weight[far_tap], ((1,), (0,))).astype(jnp.bfloat16)
         pl.when(sends_far)(far_copy(step).start)
+        hidden[at, :] = dot(block, conv_weight[1], ((1,), (0,)))
+        gated_grad[at, :] = dot(cotangent[at, :], output_weight[...], ((1,), (1,)))
 
     @pl.loop(0, chunks)
     def _(step):
         at = rows(step)
         pl.when(takes_far)(far_copy(step).wait_recv)
-        block = activated[at, :]
-        near = dot(block, conv_weight[near_tap], ((1,), (0,))) + far_in[at, :].astype(jnp.float32)
+        near = dot(activated[at, :], conv_weight[near_tap], ((1,), (0,))) + far_in[at, :].astype(jnp.float32)
         near_out[at, :] = near.astype(jnp.bfloat16)
         near_copy(step).start()
-        hidden[at, :] = dot(block, conv_weight[1], ((1,), (0,)))
-        gated_grad[at, :] = dot(cotangent[at, :], output_weight[...], ((1,), (1,)))
 
     @pl.loop(0, chunks)
     def _(step):
@@ -156,11 +155,13 @@
     def part(batch, side):
         return 3 - 2 * side if batch == 0 else 2 * side
 
-    def contribution(index, left, right):
+    def contribution(index, right):
         @pl.loop(0, channels // tile)
         def _(step):
-            at = rows(step)
-            mine[index, at, :] = dot(left[:, at], right[...], ((0,), (0,))).astype(jnp.bfloat16)
+            at = rows(step, tile)
+            mine[index, at, :] = dot(transposed[at, :], right[...], ((1,), (0,))).astype(
+                jnp.bfloat16
+            )
 
     def start_pair(batch):
         copy = pltpu.make_async_remote_copy(
@@ -214,38 +215,43 @@
         copy.start()
         return copy
 
-    contribution(3, cotangent, gated)
-    contribution(1, activated, hidden_grad)
+    @pl.loop(0, channels // tile)
+    def _(step):
+        at = rows(step, tile)
+        mine[3, at, :] = dot(cotangent[:, at], gated[...], ((0,), (0,))).astype(jnp.bfloat16)
+        transposed[at, :] = activated[:, at].T
+
+    contribution(1, hidden_grad)
     pair0 = start_pair(0)
-
-    @pl.loop(0, chunks)
-    def _(step):
-        at = rows(step)
+    pair0.wait_recv()
+    scatter0 = start_scatter(0)
+
+    @pl.loop(0, bins // tile)
+    def _(step):
+        at = rows(step, tile)
         block_out[at, :] = (
             signal[at, :].astype(jnp.float32)
             + dot(gated[at, :], output_weight[...], ((1,), (0,)))
         ).astype(jnp.bfloat16)
 
-    pair0.wait_recv()
-    scatter0 = start_scatter(0)
-
-    @pl.loop(0, chunks)
-    def _(step):
-        pl.when(has_after)(down_copy(step).wait_recv)
-        pl.when(has_before)(up_copy(step).wait_recv)
-
-    contribution(0, activated, later)
-    contribution(2, activated, earlier)
-    pair1 = start_pair(1)
     for copy in scatter0:
         copy.wait_recv()
     gather0 = start_gather(0)
+
+    @pl.loop(0, chunks)
+    def _(step):
+        pl.when(has_after)(down_copy(step).wait_recv)
+        pl.when(has_before)(up_copy(step).wait_recv)
+
+    contribution(0, later)
+    contribution(2, earlier)
+    pair1 = start_pair(1)
     pair1.wait_recv()
     scatter1 = start_scatter(1)
 
-    @pl.loop(0, chunks)
-    def _(step):
-        at = rows(step)
+    @pl.loop(0, bins // tile)
+    def _(step):
+        at = rows(step, tile)
         signal_f, inverse_rms, normed = normalized(at)
         input_gradient = (
             dot(hidden_grad[at, :], conv_weight[1], ((1,), (1,)))
@@ -289,7 +295,7 @@
     chips = devices // 2
     bins, channels = signal.shape
     width = output_weight.shape[0]
-    chunks = bins // 256
+    chunks = bins // 128
     bf16, f32 = jnp.bfloat16, jnp.float32
     vmem = pl.BlockSpec(memory_space=pltpu.VMEM)
     dma = pltpu.SemaphoreType.DMA
@@ -306,7 +312,8 @@
         in_specs=[vmem] * 5,
         out_specs=(vmem,) * 4,
         scratch_shapes=[
-            pltpu.VMEM((bins, channels), bf16), wide, wide, narrow, narrow,
+            pltpu.VMEM((bins, channels), bf16), pltpu.VMEM((channels, bins), bf16),
+            wide, wide, narrow, narrow,
             narrow, narrow, narrow, narrow, narrow, narrow,
             pltpu.VMEM((4, channels, width), bf16),
             pltpu.VMEM((2, channels, width), bf16),

time: 126 us -> 125 us (level)
  no operation moved by 1% of the time
where the time goes in v4:
time: 125 us
  Pallas kernels  116 us (93%)
  local copies, waits for them, and re-layouts  5.05 us (4%)
  other arithmetic  3.5 us (3%)
    pallas_call x1, Pallas kernels, run_whole_block(): pl.pallas_call(functools.partial(whole_block, devices), out_shape=(jax.Sh...  116 us
    unnamed x5, local copies, waits for them, and re-layouts  4.36 us
    mul x1, other arithmetic, shards(): grads[:3].astype(jnp.float32) * (1.0 / math.sqrt(local_bins * devices))  3.5 us

profile of v4, /device:TPU:31, one launch (start us, length us, event | category | flops | bytes accessed | tf_op | source)
XLA Modules:
  0.0 125.0 jit_solution(12609025886919627818)
XLA Ops:
  0.6 0.7 reshape.11.norm_gain
  1.3 0.0 copy-start
  1.3 1.1 copy-done
  2.4 115.8 %whole_block.1 = (bf16[1024,768]{1,0:T(8,128)(2,1)S(1)}, bf16[1024,768]{1,0:T(8,128)(2,1)S(1)}, bf16[4,768,384]{2,1,0:T(8,128)(2,1)}, f32[384,768]{1,0:T(8,128)S(1)}) custom-call(bf16[1024,768]{1,0:T(8,128)(2,1)} %signal.1, bf16[1024,768]{1,0:T(8,128)(2,1)} %cotangent.1, bf16[3,768,384]{2,1,0:T(8,128)(2,1)} %conv_weight.1, bf16[384,768]{1,0:T(8,128)(2,1)S(1)} %copy-done, ...), custom_call_target="tpu_custom_call" | custom-call | tf_op jit(solution)/shard_map/whole_block/pallas_call | solution.py:304
  118.2 3.5 %convert_multiply_fusion = f32[3,768,384]{2,1,0:T(8,128)} fusion(bf16[4,768,384]{2,1,0:T(8,128)(2,1)} %get-tuple-element.10), kind=kLoop, calls=%fused_computation | loop fusion | flops 1769472 | bytes 5308416 | tf_op jit(solution)/shard_map/mul | solution.py:342
  121.7 1.1 copy.12
  122.9 1.1 copy.13
  124.0 1.0 copy.14
Async XLA Ops:
  1.3 1.1 copy-start

commit v5 on v4

--- a/solution.py
+++ b/solution.py
@@ -48,6 +48,7 @@
     me = lax.axis_index("seq")
     chip, core = me // 2, me % 2
     sibling = chip * 2 + 1 - core
+    partner = {"seq": (chip + 1 - 2 * lax.rem(chip, 2)) * 2 + core}
     odd = lax.rem(me // stride, 2)
     step_sign = 2 * odd - 1
     far_tap, near_tap = 2 - 2 * odd, 2 * odd
@@ -195,12 +196,28 @@
         for distance in range(1, chips):
             total = total + pieces[batch, distance - 1].astype(jnp.float32)
         grads[index, at, :] = total.astype(jnp.bfloat16)
+        hops = [peer(2 * k)[1] for k in range(1, chips // 2)] + [partner]
         copies = []
-        for distance in range(1, chips):
+        for slot, device in enumerate(hops):
             copy = pltpu.make_async_remote_copy(
                 grads.at[index, at], grads.at[index, at],
-                gather_send.at[batch, distance - 1], gather_recv.at[batch, distance - 1],
-                device_id=peer(distance)[1],
+                gather_send.at[batch, slot], gather_recv.at[batch, slot], device_id=device,
+            )
+            copy.start()
+            copies.append(copy)
+        return copies
+
+    def pass_on(batch, arriving):
+        index = part(batch, core)
+        copies = arriving[chips // 2 - 1 :]
+        for k in range(1, chips // 2):
+            arriving[k - 1].wait_recv()
+            other = lax.rem(chip + chips - 2 * k, chips)
+            at = pl.ds(pl.multiple_of(other * piece, piece), piece)
+            slot = chips // 2 - 1 + k
+            copy = pltpu.make_async_remote_copy(
+                grads.at[index, at], grads.at[index, at],
+                gather_send.at[batch, slot], gather_recv.at[batch, slot], device_id=partner,
             )
             copy.start()
             copies.append(copy)
@@ -237,6 +254,7 @@
     for copy in scatter0:
         copy.wait_recv()
     gather0 = start_gather(0)
+    passed0 = pass_on(0, gather0)
 
     @pl.loop(0, chunks)
     def _(step):
@@ -267,19 +285,22 @@
             - signal_f * cubed * inner
         ).astype(jnp.bfloat16)
 
-    for copy in gather0:
+    for copy in passed0:
         copy.wait_recv()
     back0 = start_back(0)
     for copy in scatter1:
         copy.wait_recv()
     gather1 = start_gather(1)
+    passed1 = pass_on(1, gather1)
     back0.wait_recv()
     output_grad[...] = grads[3].astype(jnp.float32).T * grad_scale
-    for copy in gather1:
+    for copy in passed1:
         copy.wait_recv()
     back1 = start_back(1)
     back1.wait_recv()
-    for copy in [pair0, pair1, back0, back1] + scatter0 + scatter1 + gather0 + gather1:
+    for copy in [pair0, pair1, back0, back1] + scatter0 + scatter1:
+        copy.wait_send()
+    for copy in gather0[:-1] + passed0 + gather1[:-1] + passed1:
         copy.wait_send()
 
     @pl.loop(0, chunks)

time: 125 us -> 127 us (1.016)
  the two profiles are of different devices: /device:TPU:31 before, /device:TPU:0 now
where the time goes in v5:
time: 127 us
  Pallas kernels  118 us (93%)
  local copies, waits for them, and re-layouts  5.05 us (4%)
  other arithmetic  3.5 us (3%)
    pallas_call x1, Pallas kernels, run_whole_block(): pl.pallas_call(functools.partial(whole_block, devices), out_shape=(jax.Sh...  118 us
    unnamed x5, local copies, waits for them, and re-layouts  4.36 us
    mul x1, other arithmetic, shards(): grads[:3].astype(jnp.float32) * (1.0 / math.sqrt(local_bins * devices))  3.5 us

profile of v5, /device:TPU:0, one launch (start us, length us, event | category | flops | bytes accessed | tf_op | source)
XLA Modules:
  0.0 126.9 jit_solution(323911158625009329)
XLA Ops:
  0.6 0.7 reshape.11.norm_gain
  1.3 0.0 copy-start
  1.3 1.1 copy-done
  2.4 117.7 %whole_block.1 = (bf16[1024,768]{1,0:T(8,128)(2,1)S(1)}, bf16[1024,768]{1,0:T(8,128)(2,1)S(1)}, bf16[4,768,384]{2,1,0:T(8,128)(2,1)}, f32[384,768]{1,0:T(8,128)S(1)}) custom-call(bf16[1024,768]{1,0:T(8,128)(2,1)} %signal.1, bf16[1024,768]{1,0:T(8,128)(2,1)} %cotangent.1, bf16[3,768,384]{2,1,0:T(8,128)(2,1)} %conv_weight.1, bf16[384,768]{1,0:T(8,128)(2,1)S(1)} %copy-done, ...), custom_call_target="tpu_custom_call" | custom-call | tf_op jit(solution)/shard_map/whole_block/pallas_call | solution.py:325
  120.1 3.5 %convert_multiply_fusion = f32[3,768,384]{2,1,0:T(8,128)} fusion(bf16[4,768,384]{2,1,0:T(8,128)(2,1)} %get-tuple-element.10), kind=kLoop, calls=%fused_computation | loop fusion | flops 1769472 | bytes 5308416 | tf_op jit(solution)/shard_map/mul | solution.py:363
  123.6 1.1 copy.12
  124.8 1.1 copy.13
  125.9 1.0 copy.14
Async XLA Ops:
  1.3 1.1 copy-start
